TPU v7x, 32 devices: a whole 2x2x4 slice. The times are simulated.
32 devices in a mesh: pairs: 2 (over y), ctx: 8 (over z, x), head: 2 (over core).
Axes of the slice: x: 2, y: 2, z: 4, core: 2. Of those that a mesh axis runs over, the one named last changes fastest.
Arguments:
- hidden: bfloat16 [16, 2, 8192], P(('pairs', 'ctx')), parts along dimension 0, may hold values from -6 to 6
- wq: bfloat16 [8192, 4096], P('ctx', 'head'), may hold values from -0.0625 to 0.0625
- wkv: bfloat16 [2, 8192, 512], P(None, 'ctx', 'head'), may hold values from -0.0625 to 0.0625
- bias_q: bfloat16 [4096], P('head'), may hold values from -5.2 to 5.2
- bias_kv: bfloat16 [2, 512], P(None, 'head'), may hold values from -5.2 to 5.2
- key_value_cache: bfloat16 [2, 8192, 512], P(None, ('pairs', 'ctx'), 'head'), parts along dimension 1, may hold values from -46 to 46, as said below
- prompt_len: int32 [2], P('pairs'), parts along dimension 0, may hold values from 512 to 4096
- resp_len: int32 [4], P('pairs'), parts along dimension 0, may hold values from 2 to 8
Outputs:
- attn_out: bfloat16 [16, 2, 4096], P(('pairs', 'ctx'), None, 'head'), parts along dimension 0
There are 2 independent parts, one for each index of `pairs`. A program takes and returns all parts, laid end to end along the dimension named above; an argument that names none is the same for every part. Nothing has to cross between parts.
Inputs may be any that keep to these rules, and one draw needn't show every extreme that they name: `key_value_cache`: entries beyond prompt_len are padding and must not be attended to. Prompt positions from prompt_len on are padding. Token slots of response r from resp_len[r] on are padding.
All inputs are finite; a program needn't handle non-finite values.
Results may differ from a plain program's by a relative error of at most 0.025.
Values may be sent and summed in bfloat16 or wider, within the bound.
No kernel may reach another device: no remote copies, remote signals or barrier semaphores. Data moves between devices by JAX's collectives and lax.ppermute only.
A program may use at most 64 MiB of HBM per device.

v0:
```python
import jax
import jax.numpy as jnp
from jax import lax
from jax.sharding import PartitionSpec as P

HEAD_SIZE = 128
NEG_FILL = -1e30


def shards(hidden, wq, wkv, bias_q, bias_kv, key_value_cache, prompt_len, resp_len):
    tok_dev = hidden.shape[0]
    ctx_index = lax.axis_index("ctx")
    resp_tokens = tok_dev * lax.axis_size("ctx")
    q_width = wq.shape[1]
    k_width = wkv.shape[2]
    kv_local = k_width // HEAD_SIZE
    query_group_width = q_width // k_width
    score_scale = HEAD_SIZE ** (-0.5)
    row_count = 2 * tok_dev
    columns = lax.all_to_all(hidden, "ctx", split_axis=2, concat_axis=0, tiled=True)
    flat_rows = columns.reshape(2 * resp_tokens, columns.shape[2])
    weights_all = jnp.concatenate((wq, wkv[0], wkv[1]), axis=1)
    bias_all = jnp.concatenate((bias_q, bias_kv[0], bias_kv[1])).astype(jnp.float32)
    summed = lax.psum(jnp.dot(flat_rows, weights_all, preferred_element_type=jnp.float32), "ctx")
    projected = (summed + bias_all).astype(jnp.bfloat16)
    owned = lax.dynamic_slice_in_dim(projected, ctx_index * row_count, row_count, 0)
    query_rows = projected[:, :q_width].reshape(
        2 * resp_tokens, kv_local, query_group_width, HEAD_SIZE
    )
    cache_len = key_value_cache.shape[1]
    key_block = min(512, cache_len)
    block_count = cache_len // key_block
    prompt_key_rows = key_value_cache[0].reshape(block_count, key_block, kv_local, HEAD_SIZE)
    prompt_value_rows = key_value_cache[1].reshape(block_count, key_block, kv_local, HEAD_SIZE)
    first_slot = ctx_index * cache_len
    live_limit = prompt_len[0]

    def visit(carry, inputs):
        running_max, running_sum, weighted = carry
        block_keys, block_values, block_index = inputs
        scores = (
            jnp.einsum("rgjd,kgd->grjk", query_rows, block_keys, preferred_element_type=jnp.float32)
            * score_scale
        )
        position = first_slot + block_index * key_block + lax.iota(jnp.int32, key_block)
        is_live = position < live_limit
        scores = jnp.where(is_live, scores, NEG_FILL)
        new_max = jnp.maximum(running_max, jnp.max(scores, axis=-1))
        unscaled = jnp.where(is_live, jnp.exp(scores - new_max[..., None]), 0.0)
        factor = jnp.exp(running_max - new_max)
        running_sum = running_sum * factor + jnp.sum(unscaled, axis=-1)
        weighted = weighted * factor[..., None] + jnp.einsum(
            "grjk,kgd->grjd",
            unscaled.astype(jnp.bfloat16),
            block_values,
            preferred_element_type=jnp.float32,
        )
        return ((new_max, running_sum, weighted), None)

    statistic_shape = (kv_local, 2 * resp_tokens, query_group_width)
    start_state = (
        jnp.full(statistic_shape, NEG_FILL, jnp.float32),
        jnp.zeros(statistic_shape, jnp.float32),
        jnp.zeros(statistic_shape + (HEAD_SIZE,), jnp.float32),
    )
    closing_state, unused = lax.scan(
        visit,
        start_state,
        (prompt_key_rows, prompt_value_rows, jnp.arange(block_count, dtype=jnp.int32)),
    )
    owned_q = owned[:, :q_width].reshape(tok_dev, 2, kv_local, query_group_width, HEAD_SIZE)
    fresh_key_rows = projected[:, q_width : q_width + k_width].reshape(
        resp_tokens, 2, kv_local, HEAD_SIZE
    )
    fresh_value_rows = projected[:, q_width + k_width :].reshape(
        resp_tokens, 2, kv_local, HEAD_SIZE
    )
    self_scores = (
        jnp.einsum("trgjd,urgd->gtrju", owned_q, fresh_key_rows, preferred_element_type=jnp.float32)
        * score_scale
    )
    token_pos = ctx_index * tok_dev + lax.iota(jnp.int32, tok_dev)
    key_pos = lax.iota(jnp.int32, resp_tokens)
    self_live = (key_pos[None, None, :] <= token_pos[:, None, None]) & (
        key_pos[None, None, :] < resp_len[None, :, None]
    )
    self_live = self_live[None, :, :, None, :]
    self_scores = jnp.where(self_live, self_scores, NEG_FILL)
    self_max = jnp.max(self_scores, axis=-1)
    self_weights = jnp.where(self_live, jnp.exp(self_scores - self_max[..., None]), 0.0)
    self_sum = jnp.sum(self_weights, axis=-1)
    self_acc = jnp.einsum(
        "gtrju,urgd->gtrjd",
        self_weights.astype(jnp.bfloat16),
        fresh_value_rows,
        preferred_element_type=jnp.float32,
    )
    lead_shape = (1, kv_local, resp_tokens, 2, query_group_width)
    remote_max, remote_sum, remote_acc = (
        lax.all_to_all(
            closing_state[0].reshape(lead_shape), "ctx", split_axis=2, concat_axis=0, tiled=True
        ),
        lax.all_to_all(
            closing_state[1].reshape(lead_shape), "ctx", split_axis=2, concat_axis=0, tiled=True
        ),
        lax.all_to_all(
            closing_state[2].reshape(lead_shape + (HEAD_SIZE,)),
            "ctx",
            split_axis=2,
            concat_axis=0,
            tiled=True,
        ),
    )
    overall = jnp.maximum(jnp.max(remote_max, axis=0), self_max)
    remote_factor = jnp.exp(remote_max - overall[None])
    prompt_acc = jnp.sum(remote_factor[..., None] * remote_acc, axis=0)
    prompt_total = jnp.sum(remote_factor * remote_sum, axis=0)
    self_factor = jnp.exp(self_max - overall)
    numerator = prompt_acc + self_factor[..., None] * self_acc
    denominator = prompt_total + self_factor * self_sum
    result = numerator / denominator[..., None]
    row_live = token_pos[:, None] < resp_len[None, :]
    result = jnp.where(row_live[None, :, :, None, None], result, 0.0)
    return jnp.transpose(result, (1, 2, 0, 3, 4)).reshape(tok_dev, 2, q_width).astype(jnp.bfloat16)


def solution(mesh):
    return jax.shard_map(
        shards,
        mesh=mesh,
        in_specs=(
            P(("pairs", "ctx"), None, None),
            P("ctx", "head"),
            P(None, "ctx", "head"),
            P("head"),
            P(None, "head"),
            P(None, ("pairs", "ctx"), "head"),
            P("pairs"),
            P("pairs"),
        ),
        out_specs=P(("pairs", "ctx"), None, "head"),
        check_vma=False,
    )
```

profile of v0, /device:TPU:0, one launch (start us, length us, event | category | flops | bytes accessed | tf_op | source)
XLA Modules:
  0.0 205.0 jit_solution(12979786244044143791)
XLA Ops:
  6.5 8.2 %copy.38 = bf16[1,2,8192]{1,0,2:T(2,128)(2,1)} copy(bf16[1,2,8192]{2,1,0:T(2,128)(2,1)} %param.8) | data formatting | bytes 65536 | tf_op args[0]
  14.8 0.5 broadcast.132
  15.3 0.0 copy-start
  15.3 45.3 %reduce.10 = bf16[8192,2]{1,0:T(8,128)(2,1)S(1)} reduce(bf16[8192,1,2]{2,1,0:T(2,128)(2,1)} %bitcast.123, bf16[]{:T(256)} %broadcast.132), dimensions={1}, to_apply=%bitcast.111.reduce_sub_computation | reduce | bytes 65538
  60.6 0.0 copy-start.3
  60.6 0.0 copy-start.2
  60.6 3.8 %reshape.289 = bf16[8,2,1024]{2,1,0:T(2,128)(2,1)} reshape(bf16[8192,2]{1,0:T(8,128)(2,1)S(1)} %reduce.10) | data formatting | bytes 65536
  64.4 7.3 %all-to-all-start = ((bf16[8,2,1024]{2,1,0:T(2,128)(2,1)}), bf16[8,2,1024]{2,1,0:T(2,128)(2,1)S(1)}, u32[]{:S(2)}, u32[]{:S(2)}) async-start(bf16[8,2,1024]{2,1,0:T(2,128)(2,1)} %reshape.289), calls=%async_computation | async-start | bytes 65536 | tf_op jit(solution)/shard_map/all_to_all | solution.py:20
  71.7 0.0 all-reduce.2.cloned.1.call-start
  71.8 1.1 fusion.45
  72.8 0.0 copy-done
  72.8 0.1 slice_bitcast_fusion.1
  73.6 0.0 copy-done.3
  73.6 0.1 compare_and_fusion
  73.7 0.0 copy-done.2
  73.7 4.7 %all-to-all-done = bf16[8,2,1024]{2,1,0:T(2,128)(2,1)S(1)} async-done(((bf16[8,2,1024]{2,1,0:T(2,128)(2,1)}), bf16[8,2,1024]{2,1,0:T(2,128)(2,1)S(1)}, u32[]{:S(2)}, u32[]{:S(2)}) %all-to-all-start) | async-done | bytes 32800 | tf_op jit(solution)/shard_map/all_to_all | solution.py:20
  78.4 6.3 %reshape.290 = bf16[8192,1,2]{2,1,0:T(2,128)(2,1)} reshape(bf16[8,2,1024]{2,1,0:T(2,128)(2,1)S(1)} %all-to-all-done) | data formatting | bytes 65536
  84.7 8.1 %copy.39 = bf16[1,2,8192]{2,1,0:T(2,128)(2,1)S(1)} copy(bf16[1,2,8192]{1,0,2:T(2,128)(2,1)} %bitcast.124) | data formatting | bytes 65536 | tf_op jit(solution)/shard_map/all_to_all | solution.py:20
  92.8 0.0 copy-start.1
  92.9 3.3 %fusion.6 = f32[16,2560]{1,0:T(8,128)} fusion(bf16[16,1024]{1,0:T(8,128)(2,1)S(1)} %reshape.278, bf16[1024,256]{1,0:T(8,128)(2,1)S(1)} %get-tuple-element.26, bf16[1024,256]{1,0:T(8,128)(2,1)S(1)} %get-tuple-element.25, bf16[1024,2048]{1,0:T(8,128)(2,1)} %param.9), kind=kOutput, calls=%fused_computation.6 | convolution fusion | flops 99614720 | bytes 5439488 | tf_op jit(solution)/shard_map/dot_general | solution.py:24
  96.2 0.0 all-reduce.2.cloned.1.call-update
  96.2 0.1 copy.62
  96.4 0.1 copy.61
  96.5 0.0 copy-done.1
  96.6 67.2 %all-reduce.2.cloned.1.call-done = f32[16,2560]{1,0:T(8,128)} async-done(((f32[16,2560]{1,0:T(8,128)}), f32[16,2560]{1,0:T(8,128)}) %all-reduce.2.cloned.1.call-update) | async-done | bytes 163856 | tf_op jit(solution)/shard_map/psum | solution.py:24
  163.8 0.9 add_convert_fusion
  164.7 0.3 fusion.47
  165.1 0.6 copy.44
  165.7 4.4 %all-to-all-start.1 = ((f32[1,2,8,2,8]{4,3,1,0,2:T(2,128)}), f32[1,2,8,2,8]{4,3,1,0,2:T(2,128)S(1)}, u32[]{:S(2)}, u32[]{:S(2)}) async-start(f32[1,2,8,2,8]{4,3,1,0,2:T(2,128)} %copy.44), calls=%async_computation.1 | async-start | bytes 32768 | tf_op jit(solution)/shard_map/all_to_all | solution.py:100
  170.1 0.2 fusion.18
  170.4 0.3 convolution_add_fusion
  170.6 0.1 fusion.48
  170.8 0.1 fusion.29
  170.9 0.6 copy.49
  171.5 0.6 copy.52
  172.1 4.5 %all-to-all-done.1 = f32[1,2,8,2,8]{4,3,1,0,2:T(2,128)S(1)} async-done(((f32[1,2,8,2,8]{4,3,1,0,2:T(2,128)}), f32[1,2,8,2,8]{4,3,1,0,2:T(2,128)S(1)}, u32[]{:S(2)}, u32[]{:S(2)}) %all-to-all-start.1) | async-done | bytes 1056 | tf_op jit(solution)/shard_map/all_to_all | solution.py:100
  176.6 3.3 %all-to-all-start.3 = ((f32[1,2,8,2,8]{4,3,1,0,2:T(2,128)}), f32[1,2,8,2,8]{4,3,1,0,2:T(2,128)S(1)}, u32[]{:S(2)}, u32[]{:S(2)}) async-start(f32[1,2,8,2,8]{4,3,1,0,2:T(2,128)} %copy.52), calls=%async_computation.3 | async-start | bytes 32768 | tf_op jit(solution)/shard_map/all_to_all | solution.py:103
  180.0 6.5 %all-to-all-done.3 = f32[1,2,8,2,8]{4,3,1,0,2:T(2,128)S(1)} async-done(((f32[1,2,8,2,8]{4,3,1,0,2:T(2,128)}), f32[1,2,8,2,8]{4,3,1,0,2:T(2,128)S(1)}, u32[]{:S(2)}, u32[]{:S(2)}) %all-to-all-start.3) | async-done | bytes 1056 | tf_op jit(solution)/shard_map/all_to_all | solution.py:103
  186.5 3.4 %all-to-all-start.2 = ((f32[1,2,8,2,8,128]{5,4,3,1,0,2:T(8,128)}), f32[1,2,8,2,8,128]{5,4,3,1,0,2:T(8,128)S(1)}, u32[]{:S(2)}, u32[]{:S(2)}) async-start(f32[1,2,8,2,8,128]{5,4,3,1,0,2:T(8,128)} %copy.49), calls=%async_computation.2 | async-start | bytes 262144 | tf_op jit(solution)/shard_map/all_to_all | solution.py:106
  190.0 7.2 %all-to-all-done.2 = f32[1,2,8,2,8,128]{5,4,3,1,0,2:T(8,128)S(1)} async-done(((f32[1,2,8,2,8,128]{5,4,3,1,0,2:T(8,128)}), f32[1,2,8,2,8,128]{5,4,3,1,0,2:T(8,128)S(1)}, u32[]{:S(2)}, u32[]{:S(2)}) %all-to-all-start.2) | async-done | bytes 131104 | tf_op jit(solution)/shard_map/all_to_all | solution.py:106
  197.2 0.1 fusion.24
  197.3 0.2 fusion.15
  197.5 0.6 convert_element_type.36
  (22 shorter events, 0.3 us)
Async XLA Ops:
  15.3 57.6 %copy-start = (bf16[2,1024,256]{2,1,0:T(8,128)(2,1)S(1)}, bf16[2,1024,256]{2,1,0:T(8,128)(2,1)}, u32[]{:S(2)}) copy-start(bf16[2,1024,256]{2,1,0:T(8,128)(2,1)} %param.10) | copy-start | bytes 3145732
  60.6 13.0 %copy-start.3 = (s32[2]{0:T(128)S(1)}, s32[2]{0:T(128)}, u32[]{:S(2)}) copy-start(s32[2]{0:T(128)} %param.15) | copy-start | bytes 28
  60.6 13.1 %copy-start.2 = (bf16[2,256]{1,0:T(2,128)(2,1)S(1)}, bf16[2,256]{1,0:T(2,128)(2,1)}, u32[]{:S(2)}) copy-start(bf16[2,256]{1,0:T(2,128)(2,1)} %param.12) | copy-start | bytes 3076
  64.4 14.0 %all-to-all-start = ((bf16[8,2,1024]{2,1,0:T(2,128)(2,1)}), bf16[8,2,1024]{2,1,0:T(2,128)(2,1)S(1)}, u32[]{:S(2)}, u32[]{:S(2)}) async-start(bf16[8,2,1024]{2,1,0:T(2,128)(2,1)} %reshape.289), calls=%async_computation | async-start | bytes 65536 | tf_op jit(solution)/shard_map/all_to_all | solution.py:20
  71.7 92.0 %all-reduce.2.cloned.1.call-start = ((), (), s32[]{:S(2)}) async-start(), calls=%async_computation.4 | async-start | bytes 327680 | tf_op jit(solution)/shard_map/psum | solution.py:24
  92.8 3.7 %copy-start.1 = (bf16[2048]{0:T(1024)(128)(2,1)S(1)}, bf16[2048]{0:T(1024)(128)(2,1)}, u32[]{:S(2)}) copy-start(bf16[2048]{0:T(1024)(128)(2,1)} %param.11) | copy-start | bytes 12292
  165.7 11.0 %all-to-all-start.1 = ((f32[1,2,8,2,8]{4,3,1,0,2:T(2,128)}), f32[1,2,8,2,8]{4,3,1,0,2:T(2,128)S(1)}, u32[]{:S(2)}, u32[]{:S(2)}) async-start(f32[1,2,8,2,8]{4,3,1,0,2:T(2,128)} %copy.44), calls=%async_computation.1 | async-start | bytes 32768 | tf_op jit(solution)/shard_map/all_to_all | solution.py:100
  176.6 9.9 %all-to-all-start.3 = ((f32[1,2,8,2,8]{4,3,1,0,2:T(2,128)}), f32[1,2,8,2,8]{4,3,1,0,2:T(2,128)S(1)}, u32[]{:S(2)}, u32[]{:S(2)}) async-start(f32[1,2,8,2,8]{4,3,1,0,2:T(2,128)} %copy.52), calls=%async_computation.3 | async-start | bytes 32768 | tf_op jit(solution)/shard_map/all_to_all | solution.py:103
  186.5 10.7 %all-to-all-start.2 = ((f32[1,2,8,2,8,128]{5,4,3,1,0,2:T(8,128)}), f32[1,2,8,2,8,128]{5,4,3,1,0,2:T(8,128)S(1)}, u32[]{:S(2)}, u32[]{:S(2)}) async-start(f32[1,2,8,2,8,128]{5,4,3,1,0,2:T(8,128)} %copy.49), calls=%async_computation.2 | async-start | bytes 262144 | tf_op jit(solution)/shard_map/all_to_all | solution.py:106
Sparse Core Ops, SparseCore 0:
  96.3 67.3 all-reduce.1
where the time goes:
time: 206 us; the launch traced here: 205 us
  waiting for transfers between devices  90.1 us (44%)
  other arithmetic  46.9 us (23%)
  local copies, waits for them, and re-layouts  31 us (15%)
  starting transfers between devices  18.4 us (9%)
  between operations  14.3 us (7%)
  matrix products  4.29 us (2%)
    psum x1, waiting for transfers between devices, shards(): lax.psum(jnp.dot(flat_rows, weights_all, preferred_element_type=jnp.float...  67.2 us
    unnamed x1, other arithmetic  45.3 us
    unnamed x18, local copies, waits for them, and re-layouts  19.2 us
    all_to_all x2, local copies, waits for them, and re-layouts, shards(): lax.all_to_all(hidden, 'ctx', split_axis=2, concat_axis=0, tiled=True)  8.11 us
    all_to_all x1, starting transfers between devices, shards(): lax.all_to_all(hidden, 'ctx', split_axis=2, concat_axis=0, tiled=True)  7.28 us
    all_to_all x1, waiting for transfers between devices, shards(): lax.all_to_all(closing_state[2].reshape(lead_shape + (HEAD_SIZE,)), 'ctx'...  7.2 us
    all_to_all x1, waiting for transfers between devices, shards(): lax.all_to_all(closing_state[1].reshape(lead_shape), 'ctx', split_axis=2,...  6.48 us
    all_to_all x1, waiting for transfers between devices, shards(): lax.all_to_all(hidden, 'ctx', split_axis=2, concat_axis=0, tiled=True)  4.69 us
  transfers between devices with their start and end apart: 5, of which 5 were waited for; matrix products, arithmetic and copies ran while one was open for 2% of the time, Pallas kernels for 0%

commit v1 on v0

--- a/solution.py
+++ b/solution.py
@@ -21,7 +21,9 @@
     flat_rows = columns.reshape(2 * resp_tokens, columns.shape[2])
     weights_all = jnp.concatenate((wq, wkv[0], wkv[1]), axis=1)
     bias_all = jnp.concatenate((bias_q, bias_kv[0], bias_kv[1])).astype(jnp.float32)
-    summed = lax.psum(jnp.dot(flat_rows, weights_all, preferred_element_type=jnp.float32), "ctx")
+    part = jnp.dot(flat_rows, weights_all, preferred_element_type=jnp.float32)
+    shards_2 = lax.all_gather(part, "ctx")
+    summed = jnp.sum(shards_2, axis=0)
     projected = (summed + bias_all).astype(jnp.bfloat16)
     owned = lax.dynamic_slice_in_dim(projected, ctx_index * row_count, row_count, 0)
     query_rows = projected[:, :q_width].reshape(

time: 206 us -> 177 us (0.86)
  waiting for transfers between devices: 90.1 us -> 62.9 us
    psum x1 -> x0, waiting for transfers between devices: 67.2 us -> none  [shards(): lax.psum(jnp.dot(flat_rows, weights_all, preferred_element_type=jnp.float...]
    all_gather x0 -> x1, waiting for transfers between devices: none -> 38.2 us  [shards(): shards_2 = lax.all_gather(part, 'ctx')]
    unnamed x18 -> x20, local copies, waits for them, and re-layouts: 19.2 us -> 19.2 us
where the time goes in v1:
time: 177 us; the launch traced here: 176 us
  waiting for transfers between devices  62.9 us (36%)
  other arithmetic  47.4 us (27%)
  local copies, waits for them, and re-layouts  30 us (17%)
  starting transfers between devices  17.5 us (10%)
  between operations  14.3 us (8%)
  matrix products  4.35 us (2%)
    unnamed x1, other arithmetic  45.3 us
    all_gather x1, waiting for transfers between devices, shards(): shards_2 = lax.all_gather(part, 'ctx')  38.2 us
    unnamed x20, local copies, waits for them, and re-layouts  19.2 us
    all_to_all x2, local copies, waits for them, and re-layouts, shards(): lax.all_to_all(hidden, 'ctx', split_axis=2, concat_axis=0, tiled=True)  8.11 us
    all_to_all x1, starting transfers between devices, shards(): lax.all_to_all(hidden, 'ctx', split_axis=2, concat_axis=0, tiled=True)  7.28 us
    all_to_all x1, waiting for transfers between devices, shards(): lax.all_to_all(closing_state[2].reshape(lead_shape + (HEAD_SIZE,)), 'ctx'...  7.2 us
    all_to_all x1, waiting for transfers between devices, shards(): lax.all_to_all(hidden, 'ctx', split_axis=2, concat_axis=0, tiled=True)  6.55 us
    all_to_all x1, waiting for transfers between devices, shards(): lax.all_to_all(closing_state[1].reshape(lead_shape), 'ctx', split_axis=2,...  6.48 us
  transfers between devices with their start and end apart: 5, of which 5 were waited for; matrix products, arithmetic and copies ran while one was open for 2% of the time, Pallas kernels for 0%

profile of v1, /device:TPU:0, one launch (start us, length us, event | category | flops | bytes accessed | tf_op | source)
XLA Modules:
  0.0 176.4 jit_solution(12124132653678122860)
XLA Ops:
  6.5 8.2 %copy.34 = bf16[1,2,8192]{1,0,2:T(2,128)(2,1)} copy(bf16[1,2,8192]{2,1,0:T(2,128)(2,1)} %param.8) | data formatting | bytes 65536 | tf_op args[0]
  14.8 0.5 broadcast.132
  15.3 0.0 copy-start
  15.3 45.3 %reduce.10 = bf16[8192,2]{1,0:T(8,128)(2,1)S(1)} reduce(bf16[8192,1,2]{2,1,0:T(2,128)(2,1)} %bitcast.124, bf16[]{:T(256)} %broadcast.132), dimensions={1}, to_apply=%bitcast.112.reduce_sub_computation | reduce | bytes 65538
  60.6 3.8 %reshape.290 = bf16[8,2,1024]{2,1,0:T(2,128)(2,1)} reshape(bf16[8192,2]{1,0:T(8,128)(2,1)S(1)} %reduce.10) | data formatting | bytes 65536
  64.4 7.3 %all-to-all-start = ((bf16[8,2,1024]{2,1,0:T(2,128)(2,1)}), bf16[8,2,1024]{2,1,0:T(2,128)(2,1)S(1)}, u32[]{:S(2)}, u32[]{:S(2)}) async-start(bf16[8,2,1024]{2,1,0:T(2,128)(2,1)} %reshape.290), calls=%async_computation | async-start | bytes 65536 | tf_op jit(solution)/shard_map/all_to_all | solution.py:20
  71.7 0.0 all-gather.3.cloned.1.call-start
  71.7 0.0 copy-done
  71.8 0.1 slice_bitcast_fusion.1
  71.8 6.6 %all-to-all-done = bf16[8,2,1024]{2,1,0:T(2,128)(2,1)S(1)} async-done(((bf16[8,2,1024]{2,1,0:T(2,128)(2,1)}), bf16[8,2,1024]{2,1,0:T(2,128)(2,1)S(1)}, u32[]{:S(2)}, u32[]{:S(2)}) %all-to-all-start) | async-done | bytes 32800 | tf_op jit(solution)/shard_map/all_to_all | solution.py:20
  78.4 6.3 %reshape.291 = bf16[8192,1,2]{2,1,0:T(2,128)(2,1)} reshape(bf16[8,2,1024]{2,1,0:T(2,128)(2,1)S(1)} %all-to-all-done) | data formatting | bytes 65536
  84.7 8.1 %copy.35 = bf16[1,2,8192]{2,1,0:T(2,128)(2,1)S(1)} copy(bf16[1,2,8192]{1,0,2:T(2,128)(2,1)} %bitcast.125) | data formatting | bytes 65536 | tf_op jit(solution)/shard_map/all_to_all | solution.py:20
  92.8 0.0 copy-start.1
  92.8 0.0 copy-start.3
  92.8 0.0 copy-start.2
  92.9 0.0 copy-start.4
  92.9 3.4 %fusion.6 = f32[16,2560]{1,0:T(8,128)} fusion(bf16[16,1024]{1,0:T(8,128)(2,1)S(1)} %reshape.278, bf16[1024,256]{1,0:T(8,128)(2,1)S(1)} %get-tuple-element.26, bf16[1024,256]{1,0:T(8,128)(2,1)S(1)} %get-tuple-element.25, bf16[1024,2048]{1,0:T(8,128)(2,1)} %param.9), kind=kOutput, calls=%fused_computation.6 | convolution fusion | flops 99614720 | bytes 5439488 | tf_op jit(solution)/shard_map/dot_general | solution.py:24
  96.3 0.0 all-gather.3.cloned.1.call-update
  96.3 0.0 copy-done.1
  96.4 0.1 copy.58
  96.5 0.1 copy.57
  97.3 0.0 copy-done.3
  97.4 0.0 copy-done.2
  97.4 0.0 copy-done.4
  97.4 0.1 compare_and_fusion
  97.5 38.2 %all-gather.3.cloned.1.call-done = f32[128,2560]{1,0:T(8,128)} async-done(((f32[16,2560]{1,0:T(8,128)}), f32[128,2560]{1,0:T(8,128)}) %all-gather.3.cloned.1.call-update) | async-done | bytes 1310736 | tf_op jit(solution)/shard_map/all_gather | solution.py:25
  135.7 1.4 reduce_sum.56
  137.1 0.3 fusion.47
  137.5 0.6 copy.40
  138.1 3.4 %all-to-all-start.1 = ((f32[1,2,8,2,8]{4,3,1,0,2:T(2,128)}), f32[1,2,8,2,8]{4,3,1,0,2:T(2,128)S(1)}, u32[]{:S(2)}, u32[]{:S(2)}) async-start(f32[1,2,8,2,8]{4,3,1,0,2:T(2,128)} %copy.40), calls=%async_computation.1 | async-start | bytes 32768 | tf_op jit(solution)/shard_map/all_to_all | solution.py:102
  141.5 0.2 fusion.18
  141.8 0.3 convolution_add_fusion
  142.1 0.1 fusion.48
  142.2 0.1 fusion.29
  142.3 0.7 copy.45
  143.0 0.6 copy.48
  143.6 4.5 %all-to-all-done.1 = f32[1,2,8,2,8]{4,3,1,0,2:T(2,128)S(1)} async-done(((f32[1,2,8,2,8]{4,3,1,0,2:T(2,128)}), f32[1,2,8,2,8]{4,3,1,0,2:T(2,128)S(1)}, u32[]{:S(2)}, u32[]{:S(2)}) %all-to-all-start.1) | async-done | bytes 1056 | tf_op jit(solution)/shard_map/all_to_all | solution.py:102
  148.1 3.3 %all-to-all-start.3 = ((f32[1,2,8,2,8]{4,3,1,0,2:T(2,128)}), f32[1,2,8,2,8]{4,3,1,0,2:T(2,128)S(1)}, u32[]{:S(2)}, u32[]{:S(2)}) async-start(f32[1,2,8,2,8]{4,3,1,0,2:T(2,128)} %copy.48), calls=%async_computation.3 | async-start | bytes 32768 | tf_op jit(solution)/shard_map/all_to_all | solution.py:105
  151.5 6.5 %all-to-all-done.3 = f32[1,2,8,2,8]{4,3,1,0,2:T(2,128)S(1)} async-done(((f32[1,2,8,2,8]{4,3,1,0,2:T(2,128)}), f32[1,2,8,2,8]{4,3,1,0,2:T(2,128)S(1)}, u32[]{:S(2)}, u32[]{:S(2)}) %all-to-all-start.3) | async-done | bytes 1056 | tf_op jit(solution)/shard_map/all_to_all | solution.py:105
  157.9 3.4 %all-to-all-start.2 = ((f32[1,2,8,2,8,128]{5,4,3,1,0,2:T(8,128)}), f32[1,2,8,2,8,128]{5,4,3,1,0,2:T(8,128)S(1)}, u32[]{:S(2)}, u32[]{:S(2)}) async-start(f32[1,2,8,2,8,128]{5,4,3,1,0,2:T(8,128)} %copy.45), calls=%async_computation.2 | async-start | bytes 262144 | tf_op jit(solution)/shard_map/all_to_all | solution.py:108
  161.4 7.2 %all-to-all-done.2 = f32[1,2,8,2,8,128]{5,4,3,1,0,2:T(8,128)S(1)} async-done(((f32[1,2,8,2,8,128]{5,4,3,1,0,2:T(8,128)}), f32[1,2,8,2,8,128]{5,4,3,1,0,2:T(8,128)S(1)}, u32[]{:S(2)}, u32[]{:S(2)}) %all-to-all-start.2) | async-done | bytes 131104 | tf_op jit(solution)/shard_map/all_to_all | solution.py:108
  168.6 0.1 fusion.24
  168.7 0.2 fusion.15
  168.9 0.6 convert_element_type.36
  (24 shorter events, 0.4 us)
Async XLA Ops:
  15.3 56.5 %copy-start = (bf16[2,1024,256]{2,1,0:T(8,128)(2,1)S(1)}, bf16[2,1024,256]{2,1,0:T(8,128)(2,1)}, u32[]{:S(2)}) copy-start(bf16[2,1024,256]{2,1,0:T(8,128)(2,1)} %param.10) | copy-start | bytes 3145732
  64.4 14.0 %all-to-all-start = ((bf16[8,2,1024]{2,1,0:T(2,128)(2,1)}), bf16[8,2,1024]{2,1,0:T(2,128)(2,1)S(1)}, u32[]{:S(2)}, u32[]{:S(2)}) async-start(bf16[8,2,1024]{2,1,0:T(2,128)(2,1)} %reshape.290), calls=%async_computation | async-start | bytes 65536 | tf_op jit(solution)/shard_map/all_to_all | solution.py:20
  71.7 64.0 %all-gather.3.cloned.1.call-start = ((), (), s32[]{:S(2)}) async-start(), calls=%async_computation.4 | async-start | bytes 1474560 | tf_op jit(solution)/shard_map/all_gather | solution.py:25
  92.8 3.5 %copy-start.1 = (bf16[2,512,256]{2,1,0:T(8,128)(2,1)S(1)}, bf16[2,512,256]{2,1,0:T(8,128)(2,1)}, u32[]{:S(2)}) copy-start(bf16[2,512,256]{2,1,0:T(8,128)(2,1)} %param.13) | copy-start | bytes 1572868
  92.8 4.5 %copy-start.3 = (bf16[2,256]{1,0:T(2,128)(2,1)S(1)}, bf16[2,256]{1,0:T(2,128)(2,1)}, u32[]{:S(2)}) copy-start(bf16[2,256]{1,0:T(2,128)(2,1)} %param.12) | copy-start | bytes 3076
  92.8 4.5 %copy-start.2 = (bf16[2048]{0:T(1024)(128)(2,1)S(1)}, bf16[2048]{0:T(1024)(128)(2,1)}, u32[]{:S(2)}) copy-start(bf16[2048]{0:T(1024)(128)(2,1)} %param.11) | copy-start | bytes 12292
  92.9 4.5 %copy-start.4 = (s32[2]{0:T(128)S(1)}, s32[2]{0:T(128)}, u32[]{:S(2)}) copy-start(s32[2]{0:T(128)} %param.15) | copy-start | bytes 28
  138.1 10.0 %all-to-all-start.1 = ((f32[1,2,8,2,8]{4,3,1,0,2:T(2,128)}), f32[1,2,8,2,8]{4,3,1,0,2:T(2,128)S(1)}, u32[]{:S(2)}, u32[]{:S(2)}) async-start(f32[1,2,8,2,8]{4,3,1,0,2:T(2,128)} %copy.40), calls=%async_computation.1 | async-start | bytes 32768 | tf_op jit(solution)/shard_map/all_to_all | solution.py:102
  148.1 9.9 %all-to-all-start.3 = ((f32[1,2,8,2,8]{4,3,1,0,2:T(2,128)}), f32[1,2,8,2,8]{4,3,1,0,2:T(2,128)S(1)}, u32[]{:S(2)}, u32[]{:S(2)}) async-start(f32[1,2,8,2,8]{4,3,1,0,2:T(2,128)} %copy.48), calls=%async_computation.3 | async-start | bytes 32768 | tf_op jit(solution)/shard_map/all_to_all | solution.py:105
  157.9 10.7 %all-to-all-start.2 = ((f32[1,2,8,2,8,128]{5,4,3,1,0,2:T(8,128)}), f32[1,2,8,2,8,128]{5,4,3,1,0,2:T(8,128)S(1)}, u32[]{:S(2)}, u32[]{:S(2)}) async-start(f32[1,2,8,2,8,128]{5,4,3,1,0,2:T(8,128)} %copy.45), calls=%async_computation.2 | async-start | bytes 262144 | tf_op jit(solution)/shard_map/all_to_all | solution.py:108
Sparse Core Ops, SparseCore 0:
  96.4 39.2 all-gather.2
